TPU v7x, 32 devices: a whole 2x2x4 slice. The times are simulated.
32 devices in a mesh: gx: 4 (over y, core), yz: 8 (over z, x).
Axes of the slice: x: 2, y: 2, z: 4, core: 2. Of those that a mesh axis runs over, the one named last changes fastest.
Arguments:
- composition: float32 [4096, 20, 128], P(('gx', 'yz')), may hold values from -6 to 6
- particle_mass: float32 [4096, 128], P(('gx', 'yz')), may hold values from 0.5 to 2
- mixing_rate: float32 [4096, 128], P(('gx', 'yz')), may hold values from 0.2 to 3
- cell_index: int32 [4096, 128], P(('gx', 'yz')), may hold values from 0 to 4095, as said below
- section_counts: int32 [4096], P(('gx', 'yz')), may hold values from 1 to 6, as said below
- block_shuffle: int32 [32, 128], P(('gx', 'yz')), may hold values from 0 to 127, as said below
- batch_inverse: float32 [32, 20, 20], P(('gx', 'yz')), may hold values from -1.25 to 1.25
- rate_exponents: float32 [84, 20], replicated, may hold values from -1.25 to 1.25
- stoichiometry: float32 [20, 84], replicated, may hold values from -0.625 to 0.625
Outputs:
- reacted: float32 [4096, 20, 128], P(('gx', 'yz'))
Inputs may be any that keep to these rules, and one draw needn't show every extreme that they name: `cell_index`: A particle of the device at index i of gx and j of yz (d = i * 8 + j) lies in slab i - 1, i or i + 1, slab s holding cells s * 128 * 8 to (s + 1) * 128 * 8 - 1; that device's first 128 particles lie one each in cells d * 128 to d * 128 + 127. `section_counts`: some block has exactly 6 sections. `block_shuffle`: each row is a permutation of 0 to 127.
All inputs are finite; a program needn't handle non-finite values.
Results may differ from a plain program's by a relative error of at most 0.0011.
Values sent between devices are 32-bit elements; how exact they have to be, the bound alone decides.
No kernel may reach another device: no remote copies, remote signals or barrier semaphores. Data moves between devices by JAX's collectives and lax.ppermute only.
A program may use at most 128 MiB of HBM per device.

v0:
```python
import jax
import jax.numpy as jnp
from jax import lax
from jax.sharding import PartitionSpec as P

CELL_DEV = 128
step_size = 0.25


def extended_2(cells, sides, width):
    for axis, dim in sides:
        count = lax.axis_size(axis)
        ends = count - 1
        head = lax.slice_in_dim(cells, 0, width, axis=dim)
        tail = lax.slice_in_dim(cells, cells.shape[dim] - width, cells.shape[dim], axis=dim)
        cells = jnp.concatenate(
            [
                lax.ppermute(tail, axis, [(i, (i + 1) % count) for i in range(ends)]),
                cells,
                lax.ppermute(head, axis, [((i + 1) % count, i) for i in range(ends)]),
            ],
            axis=dim,
        )
    return cells


def section_update(current, matrices, rate_exponents, stoichiometry):
    progress = jnp.tanh(
        jnp.einsum("rj,bjk->brk", rate_exponents, current, precision=lax.Precision.HIGHEST)
    )
    forcing = jnp.einsum("ir,brk->bik", stoichiometry, progress, precision=lax.Precision.HIGHEST)
    return jnp.einsum("bij,bjk->bik", matrices, forcing, precision=lax.Precision.HIGHEST)


def advance_blocks(current, counts, matrices, rate_exponents, stoichiometry):
    ordering = jnp.argsort(-counts, stable=True)
    restore = jnp.argsort(ordering, stable=True)
    current = current[ordering]
    counts = counts[ordering]
    matrices = matrices[ordering]
    batch_width = min(current.shape[0], 64)

    def one_section(section_index, current):
        active = jnp.sum((counts > section_index).astype(jnp.int32))
        batches = (active + batch_width - 1) // batch_width

        def one_batch(number, current):
            offset = number * batch_width
            chosen = lax.dynamic_slice_in_dim(current, offset, batch_width, 0)
            chosen_matrices = lax.dynamic_slice_in_dim(matrices, offset, batch_width, 0)
            chosen_counts = lax.dynamic_slice_in_dim(counts, offset, batch_width, 0)
            updated = chosen + step_size * section_update(
                chosen, chosen_matrices, rate_exponents, stoichiometry
            )
            chosen = jnp.where((chosen_counts > section_index)[:, None, None], updated, chosen)
            return lax.dynamic_update_slice_in_dim(current, chosen, offset, 0)

        return lax.fori_loop(0, batches, one_batch, current)

    current = lax.fori_loop(0, jnp.max(counts), one_section, current)
    return current[restore]


def split_three(values):
    upper = values.astype(jnp.bfloat16)
    rest = values - upper.astype(jnp.float32)
    middle = rest.astype(jnp.bfloat16)
    lower = (rest - middle.astype(jnp.float32)).astype(jnp.bfloat16)
    return jnp.stack([upper, middle, lower], axis=0)


def local(
    composition,
    particle_mass,
    mixing_rate,
    cell_index,
    section_counts,
    block_shuffle,
    batch_inverse,
    rate_exponents,
    stoichiometry,
):
    block_total, species, lane_count = composition.shape
    columns = lax.axis_size("yz")
    slab_cells = CELL_DEV * columns
    first_cell = (lax.axis_index("gx") - 1) * slab_cells
    local_cell = cell_index - first_cell
    moments = species + 1
    low_width = min(256, slab_cells)
    high_count = 3 * slab_cells // low_width
    particles = block_total * lane_count
    tile = min(1024, particles)
    turns = particles // tile
    tile_blocks = tile // lane_count
    high_part = (local_cell // low_width).reshape(turns, tile)
    low_part = (local_cell % low_width).reshape(turns, tile)
    high_iota = jnp.arange(high_count, dtype=jnp.int32)
    low_iota = jnp.arange(low_width, dtype=jnp.int32)
    weighted = composition * particle_mass[:, None, :]
    values = jnp.concatenate([particle_mass[:, None, :], weighted], axis=1)
    values = (
        values.reshape(turns, tile_blocks, moments, lane_count)
        .transpose(0, 2, 1, 3)
        .reshape(turns, moments, tile)
    )

    def add_tile(number, total):
        pieces = split_three(values[number]).reshape(3 * moments, tile)
        high_table = (high_part[number][None, :] == high_iota[:, None]).astype(jnp.bfloat16)
        low_table = (low_part[number][:, None] == low_iota[None, :]).astype(jnp.bfloat16)
        spread = (pieces[:, None, :] * high_table[None, :, :]).reshape(
            3 * moments * high_count, tile
        )
        return total + jnp.dot(spread, low_table, preferred_element_type=jnp.float32)

    summed = lax.fori_loop(
        0, turns, add_tile, jnp.zeros((3 * moments * high_count, low_width), jnp.float32)
    )
    summed = summed.reshape(3, moments, 3 * slab_cells)
    partial_value = (
        (summed[0] + summed[1] + summed[2]).reshape(moments, 3, slab_cells).transpose(1, 0, 2)
    )
    extended = extended_2(partial_value, (("gx", 0),), 1)
    totals = lax.psum_scatter(
        extended[2] + extended[0] + extended[4], "yz", scatter_dimension=1, tiled=True
    )
    cell_means = totals[1:] / totals[0][None, :]
    gathered = lax.all_gather(cell_means[None], "yz", axis=2, tiled=True)
    nearby = extended_2(gathered, (("gx", 0),), 1)
    means_flat = jnp.moveaxis(nearby, 0, 1).reshape(species, 3 * slab_cells)
    mean_parts = split_three(means_flat).reshape(3, species * high_count, low_width)

    def look_tile(inputs):
        high_row, low_row = inputs
        low_table = (low_iota[:, None] == low_row[None, :]).astype(jnp.bfloat16)
        picked = jnp.dot(mean_parts[0], low_table, preferred_element_type=jnp.float32)
        picked = picked + jnp.dot(mean_parts[1], low_table, preferred_element_type=jnp.float32)
        picked = picked + jnp.dot(mean_parts[2], low_table, preferred_element_type=jnp.float32)
        high_table = (high_row[None, :] == high_iota[:, None]).astype(jnp.float32)
        return jnp.sum(picked.reshape(species, high_count, tile) * high_table[None], axis=1)

    looked = lax.map(look_tile, (high_part, low_part))
    looked = (
        looked.reshape(turns, species, tile_blocks, lane_count)
        .transpose(0, 2, 1, 3)
        .reshape(block_total, species, lane_count)
    )
    mixed_state = looked + (composition - looked) * jnp.exp(-mixing_rate)[:, None, :]
    ordering = block_shuffle[0]
    outgoing = mixed_state[ordering]
    outgoing_counts = section_counts[ordering].astype(jnp.float32)
    arrived, arrived_counts = (
        lax.all_to_all(outgoing, ("gx", "yz"), split_axis=0, concat_axis=0, tiled=True),
        lax.all_to_all(outgoing_counts, ("gx", "yz"), split_axis=0, concat_axis=0, tiled=True),
    )
    matrices = jnp.broadcast_to(batch_inverse[0], (block_total, species, species))
    reacted = advance_blocks(
        arrived, arrived_counts.astype(jnp.int32), matrices, rate_exponents, stoichiometry
    )
    returned = lax.all_to_all(reacted, ("gx", "yz"), split_axis=0, concat_axis=0, tiled=True)
    return returned[jnp.argsort(ordering, stable=True)]


def solution(mesh):
    in_specs = (
        P(("gx", "yz"), None, None),
        P(("gx", "yz"), None),
        P(("gx", "yz"), None),
        P(("gx", "yz"), None),
        P(("gx", "yz")),
        P(("gx", "yz"), None),
        P(("gx", "yz"), None, None),
        P(),
        P(),
    )
    out_specs = P(("gx", "yz"), None, None)
    return jax.shard_map(local, mesh=mesh, in_specs=in_specs, out_specs=out_specs, check_vma=False)
```

profile of v0, /device:TPU:0, one launch (start us, length us, event | category | flops | bytes accessed | tf_op | source)
XLA Modules:
  0.0 422.8 jit_solution(2543802282157748160)
XLA Ops:
  10.6 83.8 %while.68 = (s32[]{:T(128)}, f32[756,256]{1,0:T(8,128)S(1)}, f32[16,21,1024]{2,0,1:T(8,128)S(1)}, s32[16,1024]{1,0:T(8,128)}, s32[16,1024]{1,0:T(8,128)}, /*index=5*/s32[]{:T(128)}, s32[]{:T(128)}) while((s32[]{:T(128)}, f32[756,256]{1,0:T(8,128)S(1)}, f32[16,21,1024]{2,0,1:T(8,128)S(1)}, s32[16,1024]{1,0:T(8,128)}, ...), condition=%wide.region_1.2_spmd.clone, body=%wide.region_0.1_spmd.clone.sunk | while | flops 398089216 | bytes 19943576 | solution.py:116
  13.4 2.4 convolution_add_fusion.6
  18.6 2.4 convolution_add_fusion.6
  23.8 2.4 convolution_add_fusion.6
  29.1 2.4 convolution_add_fusion.6
  34.3 2.4 convolution_add_fusion.6
  39.5 2.4 convolution_add_fusion.6
  44.8 2.4 convolution_add_fusion.6
  50.0 2.4 convolution_add_fusion.6
  55.3 2.4 convolution_add_fusion.6
  60.5 2.4 convolution_add_fusion.6
  65.7 2.4 convolution_add_fusion.6
  71.0 2.4 convolution_add_fusion.6
  76.2 2.4 convolution_add_fusion.6
  81.4 2.4 convolution_add_fusion.6
  86.7 2.4 convolution_add_fusion.6
  91.9 2.4 convolution_add_fusion.6
  94.7 2.4 collective-permute-start
  98.4 4.0 collective-permute-done.1
  105.3 7.6 %all-to-all-start.1 = ((f32[32,4,1]{1,2,0:T(1,128)}), f32[32,4,1]{1,2,0:T(1,128)S(1)}, u32[]{:S(2)}, u32[]{:S(2)}) async-start(f32[32,4,1]{1,2,0:T(1,128)} %bitcast.15), calls=%async_computation.2 | async-start | bytes 32768 | tf_op jit(solution)/shard_map/all_to_all | solution.py:154
  113.0 52.3 %reduce-scatter.2.cloned.1.call-done = f32[21,128]{1,0:T(8,128)} async-done(((f32[21,1024]{1,0:T(8,128)}), f32[21,128]{1,0:T(8,128)}) %reduce-scatter.2.cloned.1.call-update) | async-done | bytes 10768 | tf_op jit(solution)/shard_map/reduce_scatter | solution.py:124
  166.7 30.5 %all-gather = f32[20,1024]{1,0:T(8,128)S(1)} all-gather(f32[20,128]{1,0:T(8,128)S(1)} %slice_divide_fusion), channel_id=2, replica_groups=mesh['gx'=4,'yz'=8] {'yz'}, dimensions={1}, use_global_device_ids=true | all-gather | bytes 92160 | tf_op jit(solution)/shard_map/all_gather | solution.py:128
  199.8 3.6 collective-permute-done.3
  203.9 47.6 %while.67 = (s32[]{:T(128)}, f32[16,20,1024]{2,1,0:T(8,128)}, s32[16,1024]{1,0:T(8,128)}, bf16[3,240,256]{2,1,0:T(8,128)(2,1)S(1)}, s32[16,1024]{1,0:T(8,128)}, /*index=5*/s32[]{:T(128)}) while((s32[]{:T(128)}, f32[16,20,1024]{2,1,0:T(8,128)}, s32[16,1024]{1,0:T(8,128)}, bf16[3,240,256]{2,1,0:T(8,128)(2,1)S(1)}, ...), condition=%wide.region_5.6_spmd.clone, body=%wide.region_3.5_spmd.clone.sunk | while | flops 379260928 | bytes 8626761 | solution.py:142
  257.1 5.7 %all-to-all-start = ((f32[128,20,128]{2,1,0:T(8,128)}), f32[128,20,128]{2,1,0:T(8,128)}, u32[]{:S(2)}, u32[]{:S(2)}) async-start(f32[128,20,128]{2,1,0:T(8,128)} %gather_fusion), calls=%async_computation.1 | async-start | bytes 3145728 | tf_op jit(solution)/shard_map/all_to_all | solution.py:153
  263.0 2.5 sort.45
  267.7 2.5 sort.46
  270.8 30.7 %all-to-all-done = f32[128,20,128]{2,1,0:T(8,128)} async-done(((f32[128,20,128]{2,1,0:T(8,128)}), f32[128,20,128]{2,1,0:T(8,128)}, u32[]{:S(2)}, u32[]{:S(2)}) %all-to-all-start) | async-done | bytes 1310752 | tf_op jit(solution)/shard_map/all_to_all | solution.py:153
  303.6 66.9 %while.66 = (s32[]{:T(128)}, f32[128,20,128]{2,1,0:T(8,128)S(1)}, s32[]{:T(128)}, s32[128]{0:T(128)S(1)}, f32[128,20,20]{2,1,0:T(8,128)S(1)}, /*index=5*/f32[84,...) while((s32[]{:T(128)}, f32[128,20,128]{2,1,0:T(8,128)S(1)}, ...), condition=%wide.region_12.13_spmd, body=%wide.region_8.12_spmd.sunk | while | flops 370115008 | bytes 10114534 | solution.py:60
  305.7 12.1 %while.69 = (s32[]{:T(128)}, f32[128,20,128]{2,1,0:T(8,128)S(1)}, s32[]{:T(128)}, s32[128]{0:T(128)S(1)}, s32[]{:T(128)}, /*index=5*/f32[128,20,20]{2,1,0:T(8,12...) while((s32[]{:T(128)}, f32[128,20,128]{2,1,0:T(8,128)S(1)}, ...), condition=%wide.region_11.11_spmd, body=%wide.region_10.10_spmd.sunk | while | flops 370114624 | bytes 10113583 | solution.py:58
  305.8 2.4 fusion.82
  311.8 2.4 fusion.82
  319.8 12.0 %while.69 = (s32[]{:T(128)}, f32[128,20,128]{2,1,0:T(8,128)S(1)}, s32[]{:T(128)}, s32[128]{0:T(128)S(1)}, s32[]{:T(128)}, /*index=5*/f32[128,20,20]{2,1,0:T(8,12...) while((s32[]{:T(128)}, f32[128,20,128]{2,1,0:T(8,128)S(1)}, ...), condition=%wide.region_11.11_spmd, body=%wide.region_10.10_spmd.sunk | while | flops 370114624 | bytes 10113583 | solution.py:58
  319.8 2.4 fusion.82
  325.8 2.4 fusion.82
  333.8 12.0 %while.69 = (s32[]{:T(128)}, f32[128,20,128]{2,1,0:T(8,128)S(1)}, s32[]{:T(128)}, s32[128]{0:T(128)S(1)}, s32[]{:T(128)}, /*index=5*/f32[128,20,20]{2,1,0:T(8,12...) while((s32[]{:T(128)}, f32[128,20,128]{2,1,0:T(8,128)S(1)}, ...), condition=%wide.region_11.11_spmd, body=%wide.region_10.10_spmd.sunk | while | flops 370114624 | bytes 10113583 | solution.py:58
  333.8 2.4 fusion.82
  339.9 2.4 fusion.82
  342.3 2.1 fusion.83
  347.9 6.0 %while.69 = (s32[]{:T(128)}, f32[128,20,128]{2,1,0:T(8,128)S(1)}, s32[]{:T(128)}, s32[128]{0:T(128)S(1)}, s32[]{:T(128)}, /*index=5*/f32[128,20,20]{2,1,0:T(8,12...) while((s32[]{:T(128)}, f32[128,20,128]{2,1,0:T(8,128)S(1)}, ...), condition=%wide.region_11.11_spmd, body=%wide.region_10.10_spmd.sunk | while | flops 370114624 | bytes 10113583 | solution.py:58
  347.9 2.4 fusion.82
  355.9 6.0 %while.69 = (s32[]{:T(128)}, f32[128,20,128]{2,1,0:T(8,128)S(1)}, s32[]{:T(128)}, s32[128]{0:T(128)S(1)}, s32[]{:T(128)}, /*index=5*/f32[128,20,20]{2,1,0:T(8,12...) while((s32[]{:T(128)}, f32[128,20,128]{2,1,0:T(8,128)S(1)}, ...), condition=%wide.region_11.11_spmd, body=%wide.region_10.10_spmd.sunk | while | flops 370114624 | bytes 10113583 | solution.py:58
  355.9 2.4 fusion.82
  363.9 6.0 %while.69 = (s32[]{:T(128)}, f32[128,20,128]{2,1,0:T(8,128)S(1)}, s32[]{:T(128)}, s32[128]{0:T(128)S(1)}, s32[]{:T(128)}, /*index=5*/f32[128,20,20]{2,1,0:T(8,12...) while((s32[]{:T(128)}, f32[128,20,128]{2,1,0:T(8,128)S(1)}, ...), condition=%wide.region_11.11_spmd, body=%wide.region_10.10_spmd.sunk | while | flops 370114624 | bytes 10113583 | solution.py:58
  363.9 2.4 fusion.82
  372.5 2.7 all-to-all-start.2
  375.2 2.5 sort.47
  377.7 36.1 %all-to-all-done.2 = f32[128,20,128]{2,1,0:T(8,128)S(1)} async-done(((f32[128,20,128]{2,1,0:T(8,128)}), f32[128,20,128]{2,1,0:T(8,128)S(1)}, u32[]{:S(2)}, u32[]{:S(2)}) %all-to-all-start.2) | async-done | bytes 1310752 | tf_op jit(solution)/shard_map/all_to_all | solution.py:160
  (443 shorter events, 152.0 us)
Async XLA Ops:
  6.5 96.8 %copy-start = (s32[128]{0:T(128)S(1)}, s32[128]{0:T(128)}, u32[]{:S(2)}) copy-start(s32[128]{0:T(128)} %param.21) | copy-start | bytes 1540
  6.5 158.7 %reduce-scatter.2.cloned.1.call-start = ((), (), s32[]{:S(2)}) async-start(), calls=%async_computation.4 | async-start | bytes 110592 | tf_op jit(solution)/shard_map/reduce_scatter | solution.py:124
  6.5 3.6 copy-start.6
  10.6 1.1 copy-start.4
  13.4 2.4 copy-start.5
  15.8 1.1 copy-start.4
  18.6 2.4 copy-start.5
  21.0 1.1 copy-start.4
  23.8 2.4 copy-start.5
  26.3 1.1 copy-start.4
  29.1 2.4 copy-start.5
  31.5 1.1 copy-start.4
  34.3 2.4 copy-start.5
  36.7 1.1 copy-start.4
  39.5 2.4 copy-start.5
  42.0 1.1 copy-start.4
  44.8 2.4 copy-start.5
  47.2 1.1 copy-start.4
  50.0 2.4 copy-start.5
  52.5 1.1 copy-start.4
  55.2 2.4 copy-start.5
  57.7 1.1 copy-start.4
  60.5 2.4 copy-start.5
  62.9 1.1 copy-start.4
  65.7 2.4 copy-start.5
  68.2 1.1 copy-start.4
  71.0 2.4 copy-start.5
  73.4 1.1 copy-start.4
  76.2 2.4 copy-start.5
  78.6 1.1 copy-start.4
  81.4 2.4 copy-start.5
  83.9 1.1 copy-start.4
  86.7 2.4 copy-start.5
  89.1 1.1 copy-start.4
  91.9 2.4 copy-start.5
  94.4 9.0 %copy-start.9 = (s32[1,128]{1,0:T(1,128)S(1)}, s32[1,128]{1,0:T(1,128)}, u32[]{:S(2)}) copy-start(s32[1,128]{1,0:T(1,128)} %param.22) | copy-start | bytes 1540
  94.4 105.4 %copy-start.7 = (f32[128,128]{1,0:T(8,128)S(1)}, f32[128,128]{1,0:T(8,128)}, u32[]{:S(2)}) copy-start(f32[128,128]{1,0:T(8,128)} %param.19) | copy-start | bytes 196612
  94.7 3.7 collective-permute-start
  97.1 5.3 %collective-permute-start.1 = (f32[1,21,1024]{2,0,1:T(1,128)S(1)}, f32[1,21,1024]{2,0,1:T(1,128)S(1)}, u32[]{:S(2)}, u32[]{:S(2)}) collective-permute-start(f32[1,21,1024]{2,0,1:T(1,128)S(1)} %get-tuple-element.518), channel_id=1, source_target_pairs={{8,0},{16,8},{24,16},{9,1},{17,9},{25,17},{10,2},{18,10},{26,18},{... | collective-permute-start | bytes 258056 | tf_op jit(solution)/shard_map/ppermute | solution.py:20
  105.3 151.8 %all-to-all-start.1 = ((f32[32,4,1]{1,2,0:T(1,128)}), f32[32,4,1]{1,2,0:T(1,128)S(1)}, u32[]{:S(2)}, u32[]{:S(2)}) async-start(f32[32,4,1]{1,2,0:T(1,128)} %bitcast.15), calls=%async_computation.2 | async-start | bytes 32768 | tf_op jit(solution)/shard_map/all_to_all | solution.py:154
  197.2 2.6 collective-permute-start.2
  198.5 4.9 %collective-permute-start.3 = (f32[1,20,1024]{2,1,0:T(8,128)S(1)}, f32[1,20,1024]{2,1,0:T(8,128)S(1)}, u32[]{:S(2)}, u32[]{:S(2)}) collective-permute-start(f32[1,20,1024]{2,1,0:T(8,128)S(1)} %bitcast.102), channel_id=1, source_target_pairs={{8,0},{16,8},{24,16},{9,1},{17,9},{25,17},{10,2},{18,10},{26,18},{... | collective-permute-start | bytes 245768 | tf_op jit(solution)/shard_map/ppermute | solution.py:20
  253.0 1.3 copy-start.3
  257.1 5.7 %copy-start.8 = (f32[1,20,20]{2,0,1:T(1,128)S(1)}, f32[1,20,20]{2,0,1:T(1,128)}, u32[]{:S(2)}) copy-start(f32[1,20,20]{2,0,1:T(1,128)} %param.23) | copy-start | bytes 4804
  257.1 44.4 %all-to-all-start = ((f32[128,20,128]{2,1,0:T(8,128)}), f32[128,20,128]{2,1,0:T(8,128)}, u32[]{:S(2)}, u32[]{:S(2)}) async-start(f32[128,20,128]{2,1,0:T(8,128)} %gather_fusion), calls=%async_computation.1 | async-start | bytes 3145728 | tf_op jit(solution)/shard_map/all_to_all | solution.py:153
  270.8 32.8 %copy-start.1 = (f32[84,20]{0,1:T(8,128)S(1)}, f32[84,20]{0,1:T(8,128)}, u32[]{:S(2)}) copy-start(f32[84,20]{0,1:T(8,128)} %param.24) | copy-start | bytes 20164
  270.8 32.8 %copy-start.2 = (f32[20,84]{1,0:T(8,128)S(1)}, f32[20,84]{1,0:T(8,128)}, u32[]{:S(2)}) copy-start(f32[20,84]{1,0:T(8,128)} %param.25) | copy-start | bytes 20164
  372.5 41.4 %all-to-all-start.2 = ((f32[128,20,128]{2,1,0:T(8,128)}), f32[128,20,128]{2,1,0:T(8,128)S(1)}, u32[]{:S(2)}, u32[]{:S(2)}) async-start(f32[128,20,128]{2,1,0:T(8,128)} %gather_fusion.5), calls=%async_computation.3 | async-start | bytes 3145728 | tf_op jit(solution)/shard_map/all_to_all | solution.py:160
Sparse Core Ops, SparseCore 0:
  103.4 61.7 reduce-scatter.1
where the time goes:
time: 427 us; the launch traced here: 423 us
  waiting for transfers between devices  127 us (30%)
  matrix products  109 us (26%)
  local copies, waits for them, and re-layouts  83 us (19%)
  blocking collectives  30.5 us (7%)
  other arithmetic  26.1 us (6%)
  starting transfers between devices  22.2 us (5%)
  between operations  13.8 us (3%)
  loops' own time  11.2 us (3%)
    reduce_scatter x1, waiting for transfers between devices, local(): lax.psum_scatter(extended[2] + extended[0] + extended[4], 'yz', scatter_d...  52.3 us
    dot_general x16, matrix products, add_tile(): jnp.dot(spread, low_table, preferred_element_type=jnp.float32)  38.6 us
    all_to_all x1, waiting for transfers between devices, local(): lax.all_to_all(reacted, ('gx', 'yz'), split_axis=0, concat_axis=0, tiled=...  36.1 us
    all_to_all x1, waiting for transfers between devices, local(): lax.all_to_all(outgoing, ('gx', 'yz'), split_axis=0, concat_axis=0, tiled...  30.7 us
    all_gather x1, blocking collectives, local(): gathered = lax.all_gather(cell_means[None], 'yz', axis=2, tiled=True)  30.5 us
    mul x32, local copies, waits for them, and re-layouts, add_tile(): pieces[:, None, :] * high_table[None, :, :]  24.4 us
    dot_general x9, matrix products, section_update(): jnp.einsum('rj,bjk->brk', rate_exponents, current, precision=lax.Precisio...  21.9 us
    dot_general x9, matrix products, section_update(): jnp.einsum('ir,brk->bik', stoichiometry, progress, precision=lax.Precisio...  18.7 us
  transfers between devices with their start and end apart: 8, of which 5 were waited for; matrix products, arithmetic and copies ran while one was open for 16% of the time, Pallas kernels for 0%

commit v1 on v0

--- a/solution.py
+++ b/solution.py
@@ -125,7 +125,7 @@
         extended[2] + extended[0] + extended[4], "yz", scatter_dimension=1, tiled=True
     )
     cell_means = totals[1:] / totals[0][None, :]
-    gathered = lax.all_gather(cell_means[None], "yz", axis=2, tiled=True)
+    gathered = jnp.concatenate(lax.all_gather(cell_means[None], "yz"), axis=2)
     nearby = extended_2(gathered, (("gx", 0),), 1)
     means_flat = jnp.moveaxis(nearby, 0, 1).reshape(species, 3 * slab_cells)
     mean_parts = split_three(means_flat).reshape(3, species * high_count, low_width)

time: 427 us -> 427 us (level)
  no operation moved by 1% of the time
where the time goes in v1:
time: 427 us; the launch traced here: 423 us
  waiting for transfers between devices  127 us (30%)
  matrix products  109 us (26%)
  local copies, waits for them, and re-layouts  82.8 us (19%)
  blocking collectives  30.5 us (7%)
  other arithmetic  26.3 us (6%)
  starting transfers between devices  22.1 us (5%)
  between operations  13.8 us (3%)
  loops' own time  11.2 us (3%)
    reduce_scatter x1, waiting for transfers between devices, local(): lax.psum_scatter(extended[2] + extended[0] + extended[4], 'yz', scatter_d...  52.3 us
    dot_general x16, matrix products, add_tile(): jnp.dot(spread, low_table, preferred_element_type=jnp.float32)  38.6 us
    all_to_all x1, waiting for transfers between devices, local(): lax.all_to_all(reacted, ('gx', 'yz'), split_axis=0, concat_axis=0, tiled=...  36.1 us
    all_to_all x1, waiting for transfers between devices, local(): lax.all_to_all(outgoing, ('gx', 'yz'), split_axis=0, concat_axis=0, tiled...  30.7 us
    all_gather x1, blocking collectives, local(): gathered = jnp.concatenate(lax.all_gather(cell_means[None], 'yz'), axis=2)  30.5 us
    mul x32, local copies, waits for them, and re-layouts, add_tile(): pieces[:, None, :] * high_table[None, :, :]  24.4 us
    dot_general x9, matrix products, section_update(): jnp.einsum('rj,bjk->brk', rate_exponents, current, precision=lax.Precisio...  21.9 us
    dot_general x9, matrix products, section_update(): jnp.einsum('ir,brk->bik', stoichiometry, progress, precision=lax.Precisio...  18.7 us
  transfers between devices with their start and end apart: 8, of which 5 were waited for; matrix products, arithmetic and copies ran while one was open for 16% of the time, Pallas kernels for 0%

profile of v1, /device:TPU:0, one launch (start us, length us, event | category | flops | bytes accessed | tf_op | source)
XLA Modules:
  0.0 422.7 jit_solution(4852000456861776144)
XLA Ops:
  10.6 83.8 %while.68 = (s32[]{:T(128)}, f32[756,256]{1,0:T(8,128)S(1)}, f32[16,21,1024]{2,0,1:T(8,128)S(1)}, s32[16,1024]{1,0:T(8,128)}, s32[16,1024]{1,0:T(8,128)}, /*index=5*/s32[]{:T(128)}, s32[]{:T(128)}) while((s32[]{:T(128)}, f32[756,256]{1,0:T(8,128)S(1)}, f32[16,21,1024]{2,0,1:T(8,128)S(1)}, s32[16,1024]{1,0:T(8,128)}, ...), condition=%wide.region_1.2_spmd.clone, body=%wide.region_0.1_spmd.clone.sunk | while | flops 398089216 | bytes 19943576 | solution.py:116
  13.4 2.4 convolution_add_fusion.6
  18.6 2.4 convolution_add_fusion.6
  23.8 2.4 convolution_add_fusion.6
  29.1 2.4 convolution_add_fusion.6
  34.3 2.4 convolution_add_fusion.6
  39.5 2.4 convolution_add_fusion.6
  44.8 2.4 convolution_add_fusion.6
  50.0 2.4 convolution_add_fusion.6
  55.3 2.4 convolution_add_fusion.6
  60.5 2.4 convolution_add_fusion.6
  65.7 2.4 convolution_add_fusion.6
  71.0 2.4 convolution_add_fusion.6
  76.2 2.4 convolution_add_fusion.6
  81.4 2.4 convolution_add_fusion.6
  86.7 2.4 convolution_add_fusion.6
  91.9 2.4 convolution_add_fusion.6
  94.7 2.4 collective-permute-start
  98.4 4.0 collective-permute-done.1
  105.3 7.6 %all-to-all-start.1 = ((f32[32,4,1]{1,2,0:T(1,128)}), f32[32,4,1]{1,2,0:T(1,128)S(1)}, u32[]{:S(2)}, u32[]{:S(2)}) async-start(f32[32,4,1]{1,2,0:T(1,128)} %bitcast.18), calls=%async_computation.2 | async-start | bytes 32768 | tf_op jit(solution)/shard_map/all_to_all | solution.py:154
  113.0 52.3 %reduce-scatter.2.cloned.1.call-done = f32[21,128]{1,0:T(8,128)} async-done(((f32[21,1024]{1,0:T(8,128)}), f32[21,128]{1,0:T(8,128)}) %reduce-scatter.2.cloned.1.call-update) | async-done | bytes 10768 | tf_op jit(solution)/shard_map/reduce_scatter | solution.py:124
  166.7 30.5 %all-gather.1 = f32[8,20,128]{2,1,0:T(8,128)S(1)} all-gather(f32[1,20,128]{2,1,0:T(8,128)S(1)} %fusion.42), channel_id=2, replica_groups=mesh['gx'=4,'yz'=8] {'yz'}, dimensions={0}, use_global_device_ids=true | all-gather | bytes 92160 | tf_op jit(solution)/shard_map/all_gather | solution.py:128
  199.9 3.5 collective-permute-done.3
  203.9 47.6 %while.67 = (s32[]{:T(128)}, f32[16,20,1024]{2,1,0:T(8,128)}, s32[16,1024]{1,0:T(8,128)}, bf16[3,240,256]{2,1,0:T(8,128)(2,1)S(1)}, s32[16,1024]{1,0:T(8,128)}, /*index=5*/s32[]{:T(128)}) while((s32[]{:T(128)}, f32[16,20,1024]{2,1,0:T(8,128)}, s32[16,1024]{1,0:T(8,128)}, bf16[3,240,256]{2,1,0:T(8,128)(2,1)S(1)}, ...), condition=%wide.region_5.6_spmd.clone, body=%wide.region_3.5_spmd.clone.sunk | while | flops 379260928 | bytes 8626761 | solution.py:142
  257.1 5.5 %all-to-all-start = ((f32[128,20,128]{2,1,0:T(8,128)}), f32[128,20,128]{2,1,0:T(8,128)}, u32[]{:S(2)}, u32[]{:S(2)}) async-start(f32[128,20,128]{2,1,0:T(8,128)} %gather_fusion), calls=%async_computation.1 | async-start | bytes 3145728 | tf_op jit(solution)/shard_map/all_to_all | solution.py:153
  262.9 2.5 sort.45
  267.5 2.5 sort.46
  270.7 30.7 %all-to-all-done = f32[128,20,128]{2,1,0:T(8,128)} async-done(((f32[128,20,128]{2,1,0:T(8,128)}), f32[128,20,128]{2,1,0:T(8,128)}, u32[]{:S(2)}, u32[]{:S(2)}) %all-to-all-start) | async-done | bytes 1310752 | tf_op jit(solution)/shard_map/all_to_all | solution.py:153
  303.4 66.9 %while.66 = (s32[]{:T(128)}, f32[128,20,128]{2,1,0:T(8,128)S(1)}, s32[]{:T(128)}, s32[128]{0:T(128)S(1)}, f32[128,20,20]{2,1,0:T(8,128)S(1)}, /*index=5*/f32[84,...) while((s32[]{:T(128)}, f32[128,20,128]{2,1,0:T(8,128)S(1)}, ...), condition=%wide.region_12.13_spmd, body=%wide.region_8.12_spmd.sunk | while | flops 370115008 | bytes 10114534 | solution.py:60
  305.6 12.1 %while.69 = (s32[]{:T(128)}, f32[128,20,128]{2,1,0:T(8,128)S(1)}, s32[]{:T(128)}, s32[128]{0:T(128)S(1)}, s32[]{:T(128)}, /*index=5*/f32[128,20,20]{2,1,0:T(8,12...) while((s32[]{:T(128)}, f32[128,20,128]{2,1,0:T(8,128)S(1)}, ...), condition=%wide.region_11.11_spmd, body=%wide.region_10.10_spmd.sunk | while | flops 370114624 | bytes 10113583 | solution.py:58
  305.6 2.4 fusion.83
  311.7 2.4 fusion.83
  319.7 12.0 %while.69 = (s32[]{:T(128)}, f32[128,20,128]{2,1,0:T(8,128)S(1)}, s32[]{:T(128)}, s32[128]{0:T(128)S(1)}, s32[]{:T(128)}, /*index=5*/f32[128,20,20]{2,1,0:T(8,12...) while((s32[]{:T(128)}, f32[128,20,128]{2,1,0:T(8,128)S(1)}, ...), condition=%wide.region_11.11_spmd, body=%wide.region_10.10_spmd.sunk | while | flops 370114624 | bytes 10113583 | solution.py:58
  319.7 2.4 fusion.83
  322.1 2.1 fusion.84
  325.7 2.4 fusion.83
  333.7 12.0 %while.69 = (s32[]{:T(128)}, f32[128,20,128]{2,1,0:T(8,128)S(1)}, s32[]{:T(128)}, s32[128]{0:T(128)S(1)}, s32[]{:T(128)}, /*index=5*/f32[128,20,20]{2,1,0:T(8,12...) while((s32[]{:T(128)}, f32[128,20,128]{2,1,0:T(8,128)S(1)}, ...), condition=%wide.region_11.11_spmd, body=%wide.region_10.10_spmd.sunk | while | flops 370114624 | bytes 10113583 | solution.py:58
  333.7 2.4 fusion.83
  339.7 2.4 fusion.83
  347.7 6.0 %while.69 = (s32[]{:T(128)}, f32[128,20,128]{2,1,0:T(8,128)S(1)}, s32[]{:T(128)}, s32[128]{0:T(128)S(1)}, s32[]{:T(128)}, /*index=5*/f32[128,20,20]{2,1,0:T(8,12...) while((s32[]{:T(128)}, f32[128,20,128]{2,1,0:T(8,128)S(1)}, ...), condition=%wide.region_11.11_spmd, body=%wide.region_10.10_spmd.sunk | while | flops 370114624 | bytes 10113583 | solution.py:58
  347.8 2.4 fusion.83
  355.8 6.0 %while.69 = (s32[]{:T(128)}, f32[128,20,128]{2,1,0:T(8,128)S(1)}, s32[]{:T(128)}, s32[128]{0:T(128)S(1)}, s32[]{:T(128)}, /*index=5*/f32[128,20,20]{2,1,0:T(8,12...) while((s32[]{:T(128)}, f32[128,20,128]{2,1,0:T(8,128)S(1)}, ...), condition=%wide.region_11.11_spmd, body=%wide.region_10.10_spmd.sunk | while | flops 370114624 | bytes 10113583 | solution.py:58
  355.8 2.4 fusion.83
  363.8 6.0 %while.69 = (s32[]{:T(128)}, f32[128,20,128]{2,1,0:T(8,128)S(1)}, s32[]{:T(128)}, s32[128]{0:T(128)S(1)}, s32[]{:T(128)}, /*index=5*/f32[128,20,20]{2,1,0:T(8,12...) while((s32[]{:T(128)}, f32[128,20,128]{2,1,0:T(8,128)S(1)}, ...), condition=%wide.region_11.11_spmd, body=%wide.region_10.10_spmd.sunk | while | flops 370114624 | bytes 10113583 | solution.py:58
  363.8 2.4 fusion.83
  372.3 2.7 all-to-all-start.2
  375.0 2.5 sort.47
  377.6 36.1 %all-to-all-done.2 = f32[128,20,128]{2,1,0:T(8,128)S(1)} async-done(((f32[128,20,128]{2,1,0:T(8,128)}), f32[128,20,128]{2,1,0:T(8,128)S(1)}, u32[]{:S(2)}, u32[]{:S(2)}) %all-to-all-start.2) | async-done | bytes 1310752 | tf_op jit(solution)/shard_map/all_to_all | solution.py:160
  (443 shorter events, 152.1 us)
Async XLA Ops:
  6.5 96.8 %copy-start = (s32[128]{0:T(128)S(1)}, s32[128]{0:T(128)}, u32[]{:S(2)}) copy-start(s32[128]{0:T(128)} %param.21) | copy-start | bytes 1540
  6.5 158.7 %reduce-scatter.2.cloned.1.call-start = ((), (), s32[]{:S(2)}) async-start(), calls=%async_computation.4 | async-start | bytes 110592 | tf_op jit(solution)/shard_map/reduce_scatter | solution.py:124
  6.5 3.6 copy-start.6
  10.6 1.1 copy-start.4
  13.4 2.4 copy-start.5
  15.8 1.1 copy-start.4
  18.6 2.4 copy-start.5
  21.0 1.1 copy-start.4
  23.8 2.4 copy-start.5
  26.3 1.1 copy-start.4
  29.1 2.4 copy-start.5
  31.5 1.1 copy-start.4
  34.3 2.4 copy-start.5
  36.7 1.1 copy-start.4
  39.5 2.4 copy-start.5
  42.0 1.1 copy-start.4
  44.8 2.4 copy-start.5
  47.2 1.1 copy-start.4
  50.0 2.4 copy-start.5
  52.5 1.1 copy-start.4
  55.2 2.4 copy-start.5
  57.7 1.1 copy-start.4
  60.5 2.4 copy-start.5
  62.9 1.1 copy-start.4
  65.7 2.4 copy-start.5
  68.2 1.1 copy-start.4
  71.0 2.4 copy-start.5
  73.4 1.1 copy-start.4
  76.2 2.4 copy-start.5
  78.6 1.1 copy-start.4
  81.4 2.4 copy-start.5
  83.9 1.1 copy-start.4
  86.7 2.4 copy-start.5
  89.1 1.1 copy-start.4
  91.9 2.4 copy-start.5
  94.4 9.0 %copy-start.9 = (s32[1,128]{1,0:T(1,128)S(1)}, s32[1,128]{1,0:T(1,128)}, u32[]{:S(2)}) copy-start(s32[1,128]{1,0:T(1,128)} %param.22) | copy-start | bytes 1540
  94.4 105.5 %copy-start.7 = (f32[128,128]{1,0:T(8,128)S(1)}, f32[128,128]{1,0:T(8,128)}, u32[]{:S(2)}) copy-start(f32[128,128]{1,0:T(8,128)} %param.19) | copy-start | bytes 196612
  94.7 3.7 collective-permute-start
  97.1 5.3 %collective-permute-start.1 = (f32[1,21,1024]{2,0,1:T(1,128)S(1)}, f32[1,21,1024]{2,0,1:T(1,128)S(1)}, u32[]{:S(2)}, u32[]{:S(2)}) collective-permute-start(f32[1,21,1024]{2,0,1:T(1,128)S(1)} %get-tuple-element.518), channel_id=1, source_target_pairs={{8,0},{16,8},{24,16},{9,1},{17,9},{25,17},{10,2},{18,10},{26,18},{... | collective-permute-start | bytes 258056 | tf_op jit(solution)/shard_map/ppermute | solution.py:20
  105.3 151.8 %all-to-all-start.1 = ((f32[32,4,1]{1,2,0:T(1,128)}), f32[32,4,1]{1,2,0:T(1,128)S(1)}, u32[]{:S(2)}, u32[]{:S(2)}) async-start(f32[32,4,1]{1,2,0:T(1,128)} %bitcast.18), calls=%async_computation.2 | async-start | bytes 32768 | tf_op jit(solution)/shard_map/all_to_all | solution.py:154
  197.2 2.6 collective-permute-start.2
  198.5 4.9 %collective-permute-start.3 = (f32[1,20,1024]{2,0,1:T(1,128)S(1)}, f32[1,20,1024]{2,0,1:T(1,128)S(1)}, u32[]{:S(2)}, u32[]{:S(2)}) collective-permute-start(f32[1,20,1024]{2,0,1:T(1,128)S(1)} %bitcast.108), channel_id=1, source_target_pairs={{8,0},{16,8},{24,16},{9,1},{17,9},{25,17},{10,2},{18,10},{26,18},{... | collective-permute-start | bytes 245768 | tf_op jit(solution)/shard_map/ppermute | solution.py:20
  253.0 1.3 copy-start.3
  257.1 5.5 %copy-start.8 = (f32[1,20,20]{2,0,1:T(1,128)S(1)}, f32[1,20,20]{2,0,1:T(1,128)}, u32[]{:S(2)}) copy-start(f32[1,20,20]{2,0,1:T(1,128)} %param.23) | copy-start | bytes 4804
  257.1 44.2 %all-to-all-start = ((f32[128,20,128]{2,1,0:T(8,128)}), f32[128,20,128]{2,1,0:T(8,128)}, u32[]{:S(2)}, u32[]{:S(2)}) async-start(f32[128,20,128]{2,1,0:T(8,128)} %gather_fusion), calls=%async_computation.1 | async-start | bytes 3145728 | tf_op jit(solution)/shard_map/all_to_all | solution.py:153
  270.6 32.8 %copy-start.1 = (f32[84,20]{0,1:T(8,128)S(1)}, f32[84,20]{0,1:T(8,128)}, u32[]{:S(2)}) copy-start(f32[84,20]{0,1:T(8,128)} %param.24) | copy-start | bytes 20164
  270.7 32.8 %copy-start.2 = (f32[20,84]{1,0:T(8,128)S(1)}, f32[20,84]{1,0:T(8,128)}, u32[]{:S(2)}) copy-start(f32[20,84]{1,0:T(8,128)} %param.25) | copy-start | bytes 20164
  372.3 41.4 %all-to-all-start.2 = ((f32[128,20,128]{2,1,0:T(8,128)}), f32[128,20,128]{2,1,0:T(8,128)S(1)}, u32[]{:S(2)}, u32[]{:S(2)}) async-start(f32[128,20,128]{2,1,0:T(8,128)} %gather_fusion.5), calls=%async_computation.3 | async-start | bytes 3145728 | tf_op jit(solution)/shard_map/all_to_all | solution.py:160
Sparse Core Ops, SparseCore 0:
  103.4 61.7 reduce-scatter.1
